TPU v7x, 512 devices: a whole 4x4x16 slice. The times are simulated.
512 devices in a mesh: dp: 16 (over y, x), tensor: 32 (over z, core).
Axes of the slice: x: 4, y: 4, z: 16, core: 2. Of those that a mesh axis runs over, the one named last changes fastest.
Arguments:
- inputs: bfloat16 [2048, 4096], P('dp', 'tensor'), may hold values from -6 to 6
- cotangent: bfloat16 [2048, 4096], P('dp', 'tensor'), may hold values from -6 to 6
- gate_w: bfloat16 [32, 24, 128, 128], P('tensor'), may hold values from -0.25 to 0.25
- up_w: bfloat16 [32, 24, 128, 128], P('tensor'), may hold values from -0.25 to 0.25
- down_w: bfloat16 [32, 24, 128, 128], P('tensor'), may hold values from -0.25 to 0.25
- gate_list: int32 [32, 24], P('tensor'), may hold values from -1 to 127, as said below
- up_list: int32 [32, 24], P('tensor'), may hold values from -1 to 127, as said below
- down_list: int32 [32, 24], P('tensor'), may hold values from -1 to 127, as said below
Outputs:
- grad_x: bfloat16 [2048, 4096], P('dp', 'tensor')
- grad_gate_w: bfloat16 [32, 24, 128, 128], P('tensor', None, 'dp')
- grad_up_w: bfloat16 [32, 24, 128, 128], P('tensor', None, 'dp')
- grad_down_w: bfloat16 [32, 24, 128, 128], P('tensor', None, 'dp')
Inputs may be any that keep to these rules, and one draw needn't show every extreme that they name: `gate_list`: row j of the list names blocks of hidden blocks j * 4 to j * 4 + 3 only; no entry appears twice in a row; live entries come first and -1 fills the rest; a row holds at most 24 live entries and some row holds exactly 24. `up_list`: as for gate_list, drawn independently. `down_list`: as for gate_list, drawn independently.
All inputs are finite; a program needn't handle non-finite values.
Results may differ from a plain program's by a relative error of at most 0.014.
Values may be sent and summed in bfloat16 or wider, within the bound.
No kernel may reach another device: no remote copies, remote signals or barrier semaphores. Data moves between devices by JAX's collectives and lax.ppermute only.
A program may use at most 64 MiB of HBM per device.

v0:
```python
import math
import jax
import jax.numpy as jnp
from jax import lax
from jax.sharding import PartitionSpec as P

D = 4096
FF = 16384
BLOCK = 128


def decode(entries, row_count):
    living = entries >= 0
    clamped = jnp.maximum(entries, 0)
    return (living, clamped // row_count, clamped % row_count)


def one_hot(block_index, width_count, living):
    return ((block_index[:, None] == jnp.arange(width_count)[None, :]) & living[:, None]).astype(
        jnp.float32
    )


def select_sum(values, table):
    return jnp.sum(values[:, :, None, :] * table[None, :, :, None], axis=1)


def project_rows(blocks_in, weights, rows_hot):
    products = jnp.einsum("tkc,kch->tkh", blocks_in, weights, preferred_element_type=jnp.float32)
    return select_sum(products, rows_hot)


def weight_term(products, grad_scale, living):
    rounded = (products * grad_scale).astype(jnp.bfloat16)
    rounded = lax.optimization_barrier(rounded)
    return (rounded.astype(jnp.float32) * living[:, None, None].astype(jnp.float32))[None]


def add_sources(received):
    return jnp.sum(received.astype(jnp.float32), axis=1)


def on_device(inputs, cotangent, gate_w, up_w, down_w, gate_list, up_list, down_list):
    tensor_size = lax.axis_size("tensor")
    hidden_rows = FF // (BLOCK * tensor_size)
    feat_blocks = D // BLOCK
    tokens_here = inputs.shape[0]
    grad_scale = 1.0 / math.sqrt(tokens_here * lax.axis_size("dp"))
    gate_live, gate_feat, gate_row = decode(gate_list[0], hidden_rows)
    up_live, up_feat, up_row = decode(up_list[0], hidden_rows)
    down_live, down_feat, down_row = decode(down_list[0], hidden_rows)
    whole_in, whole_cot = (
        lax.all_gather(inputs, "tensor", axis=1, tiled=True),
        lax.all_gather(cotangent, "tensor", axis=1, tiled=True),
    )
    input_blocks = whole_in.reshape(tokens_here, feat_blocks, BLOCK)
    gate_in = jnp.take(input_blocks, gate_feat, axis=1)
    up_in = jnp.take(input_blocks, up_feat, axis=1)
    gate_val = project_rows(gate_in, gate_w[0], one_hot(gate_row, hidden_rows, gate_live))
    up_val = project_rows(up_in, up_w[0], one_hot(up_row, hidden_rows, up_live))
    sigmoid_gate = jax.nn.sigmoid(gate_val)
    active = gate_val * sigmoid_gate
    hidden = (active * up_val).astype(jnp.bfloat16)
    cot_blocks = whole_cot.reshape(tokens_here, feat_blocks, BLOCK)
    down_cot = jnp.take(cot_blocks, down_feat, axis=1)
    hidden_down = jnp.take(hidden, down_row, axis=1)
    down_part = jnp.einsum("tkc,khc->tkh", down_cot, down_w[0], preferred_element_type=jnp.float32)
    grad_hidden = select_sum(down_part, one_hot(down_row, hidden_rows, down_live))
    down_term = weight_term(
        jnp.einsum("tkh,tkc->khc", hidden_down, down_cot, preferred_element_type=jnp.float32),
        grad_scale,
        down_live,
    )
    grad_gate = (
        grad_hidden * up_val * sigmoid_gate * (1.0 + gate_val * (1.0 - sigmoid_gate))
    ).astype(jnp.bfloat16)
    grad_up = (grad_hidden * active).astype(jnp.bfloat16)
    gate_back = jnp.take(grad_gate, gate_row, axis=1)
    up_back = jnp.take(grad_up, up_row, axis=1)
    gate_term = weight_term(
        jnp.einsum("tkc,tkh->kch", gate_in, gate_back, preferred_element_type=jnp.float32),
        grad_scale,
        gate_live,
    )
    up_term = weight_term(
        jnp.einsum("tkc,tkh->kch", up_in, up_back, preferred_element_type=jnp.float32),
        grad_scale,
        up_live,
    )
    back_gate = jnp.einsum("tkh,kch->tkc", gate_back, gate_w[0], preferred_element_type=jnp.float32)
    back_up = jnp.einsum("tkh,kch->tkc", up_back, up_w[0], preferred_element_type=jnp.float32)
    partial_sum = select_sum(back_gate, one_hot(gate_feat, feat_blocks, gate_live))
    partial_sum = partial_sum + select_sum(back_up, one_hot(up_feat, feat_blocks, up_live))
    pieces = partial_sum.astype(jnp.bfloat16)
    summed = add_sources(lax.all_to_all(pieces, "tensor", split_axis=1, concat_axis=1, tiled=True))
    grad_x = summed.astype(jnp.bfloat16)
    gate_sum, up_sum, down_sum = (
        lax.psum_scatter(
            gate_term.astype(jnp.bfloat16), "dp", scatter_dimension=2, tiled=True
        ).astype(jnp.float32),
        lax.psum_scatter(
            up_term.astype(jnp.bfloat16), "dp", scatter_dimension=2, tiled=True
        ).astype(jnp.float32),
        lax.psum_scatter(
            down_term.astype(jnp.bfloat16), "dp", scatter_dimension=2, tiled=True
        ).astype(jnp.float32),
    )
    return (
        grad_x,
        gate_sum.astype(jnp.bfloat16),
        up_sum.astype(jnp.bfloat16),
        down_sum.astype(jnp.bfloat16),
    )


def solution(mesh):
    return jax.shard_map(
        on_device,
        mesh=mesh,
        in_specs=(
            P("dp", "tensor"),
            P("dp", "tensor"),
            P("tensor", None, None, None),
            P("tensor", None, None, None),
            P("tensor", None, None, None),
            P("tensor", None),
            P("tensor", None),
            P("tensor", None),
        ),
        out_specs=(
            P("dp", "tensor"),
            P("tensor", None, "dp", None),
            P("tensor", None, "dp", None),
            P("tensor", None, "dp", None),
        ),
        check_vma=False,
    )
```

profile of v0, /device:TPU:32, one launch (start us, length us, event | category | flops | bytes accessed | tf_op | source)
XLA Modules:
  0.0 357.0 jit_solution(7031194713557921426)
XLA Ops:
  7.2 0.0 copy-start
  7.2 0.0 all-gather.5.cloned.1.call-start
  7.2 1.5 copy.56
  8.8 0.0 all-gather.5.cloned.1.call-update
  8.8 0.0 all-gather.3.cloned.1.call-start
  8.8 1.5 copy.53
  10.3 0.0 all-gather.3.cloned.1.call-update
  10.3 0.7 compare_and_fusion.4
  11.0 1.2 fusion.45
  12.3 1.2 compare_and_fusion.2
  13.5 1.2 fusion.46
  14.8 1.2 compare_and_fusion.5
  16.0 0.6 pad_clamp_fusion.2
  16.6 1.2 fusion.44
  17.8 0.1 fusion.26
  17.9 0.7 fusion.24
  18.6 66.7 %all-gather.5.cloned.1.call-done = bf16[128,4096]{0,1:T(8,128)(2,1)} async-done(((bf16[128,128]{0,1:T(8,128)(2,1)}), bf16[128,4096]{0,1:T(8,128)(2,1)}) %all-gather.5.cloned.1.call-update) | async-done | bytes 1048592 | tf_op jit(solution)/shard_map/all_gather | solution.py:53
  85.2 1.6 copy.57
  86.9 0.7 gather_fusion.1
  87.6 0.9 copy-done.2
  88.5 0.4 convolution_bitcast_fusion.3
  88.9 0.9 copy.58
  89.8 1.6 gather_fusion.2
  91.4 1.8 convolution_bitcast_fusion.2
  93.2 2.1 copy.62
  95.2 60.6 %all-gather.3.cloned.1.call-done = bf16[128,4096]{0,1:T(8,128)(2,1)} async-done(((bf16[128,128]{0,1:T(8,128)(2,1)}), bf16[128,4096]{0,1:T(8,128)(2,1)}) %all-gather.3.cloned.1.call-update) | async-done | bytes 1048592 | tf_op jit(solution)/shard_map/all_gather | solution.py:54
  155.8 1.8 copy.54
  157.6 1.6 gather_fusion
  159.2 2.1 convolution_bitcast_fusion.4
  161.3 0.9 copy.55
  162.2 1.8 multiply_reduce_fusion.4
  164.0 3.5 multiply_reduce_fusion.2
  167.5 0.2 multiply_convert_fusion.6
  167.7 0.7 gather_fusion.4
  168.4 0.7 convolution_bitcast_fusion
  169.1 0.2 copy-done.6
  169.3 0.9 copy.68
  170.2 0.8 gather_fusion.3
  171.0 2.1 convolution_bitcast_fusion.1
  173.2 0.9 copy.65
  174.1 0.0 copy-start.11
  174.1 13.1 %multiply_reduce_fusion = f32[128,32,128]{2,1,0:T(8,128)S(1)} fusion(f32[24,32]{1,0:T(8,128)S(1)} %fusion.26, f32[128,24,128]{2,1,0:T(8,128)S(1)} %copy.68), kind=kLoop, calls=%fused_computation.6 | loop fusion | flops 24641536 | bytes 3673088 | tf_op jit(solution)/shard_map/reduce_sum | solution.py:25
  187.2 13.3 %multiply_reduce_fusion.1 = f32[128,32,128]{2,1,0:T(8,128)S(1)} fusion(f32[24,32]{1,0:T(8,128)S(1)} %copy-done.11, f32[128,24,128]{2,1,0:T(8,128)S(1)} %copy.65), kind=kLoop, calls=%fused_computation.7 | loop fusion | flops 24641536 | bytes 3673088 | tf_op jit(solution)/shard_map/reduce_sum | solution.py:25
  200.6 0.5 add_convert_fusion
  201.1 1.4 copy.69
  202.5 9.0 %all-to-all-start = ((bf16[128,32,128]{2,0,1:T(8,128)(2,1)}), bf16[128,32,128]{2,0,1:T(8,128)(2,1)S(1)}, u32[]{:S(2)}, u32[]{:S(2)}) async-start(bf16[128,32,128]{2,0,1:T(8,128)(2,1)} %copy.69), calls=%async_computation | async-start | bytes 2097152 | tf_op jit(solution)/shard_map/all_to_all | solution.py:95
  211.5 0.0 all-reduce.6.cloned.1.call-start
  211.6 2.6 multiply_convert_fusion.3
  214.3 1.4 multiply_convert_fusion.5
  215.7 0.7 gather_fusion.5
  216.4 0.4 copy-done.5
  216.8 0.5 multiply_convert_fusion.1
  217.4 0.6 copy-done.9
  218.0 1.1 fusion.1
  219.1 1.1 fusion
  220.2 1.1 fusion.2
  221.3 0.0 all-reduce.6.cloned.1.call-update
  221.4 1.3 dynamic-slice
  223.3 122.1 %all-reduce.6.cloned.1.call-done = (bf16[1,24,128,128]{3,2,1,0:T(8,128)(2,1)}, bf16[1,24,128,128]{3,2,1,0:T(8,128)(2,1)}, bf16[1,24,128,128]{3,2,1,0:T(8,128)(2,1)}) async-done(((bf16[1,24,128,128]{3,2,1,0:T(8,128)(2,1)}, bf16[1,24,128,128]{3,2,1,0:T(8,128)(2,1)}, bf16[1,24,128,128]{3,2,1,0:T(8,128)(2,1)}), (bf16[1,24,128,128]{3,2,1,0:T(8,128)(2,1)}, bf16[1,24,128,128]{3,2,1,0:T(8,128)(2,1)}, ...) | async-done | bytes 2359312
  345.4 1.4 constant_dynamic-slice_fusion
  346.9 1.4 constant_dynamic-slice_fusion.1
  348.3 1.4 constant_dynamic-slice_fusion.2
  349.7 0.0 all-to-all-done
  349.7 0.8 reduce_sum.62
  (59 shorter events, 0.2 us)
Async XLA Ops:
  7.2 81.3 %copy-start = (bf16[1,24,128,128]{3,2,1,0:T(8,128)(2,1)S(1)}, bf16[1,24,128,128]{3,2,1,0:T(8,128)(2,1)}, u32[]{:S(2)}) copy-start(bf16[1,24,128,128]{3,2,1,0:T(8,128)(2,1)} %param.15) | copy-start | bytes 2359300
  7.2 78.1 %all-gather.5.cloned.1.call-start = ((), (), s32[]{:S(2)}) async-start(), calls=%async_computation.2 | async-start | bytes 1081344 | tf_op jit(solution)/shard_map/all_gather | solution.py:53
  8.8 147.0 %all-gather.3.cloned.1.call-start = ((), (), s32[]{:S(2)}) async-start(), calls=%async_computation.1 | async-start | bytes 1081344 | tf_op jit(solution)/shard_map/all_gather | solution.py:54
  11.0 76.6 %copy-start.12 = (pred[24]{0:T(512)(128)(4,1)}, pred[24]{0:T(512)(128)(4,1)S(1)}, u32[]{:S(2)}) copy-start(pred[24]{0:T(512)(128)(4,1)S(1)} %get-tuple-element.17) | copy-start | bytes 76
  11.0 157.4 %copy-start.14 = (pred[24]{0:T(512)(128)(4,1)}, pred[24]{0:T(512)(128)(4,1)S(1)}, u32[]{:S(2)}) copy-start(pred[24]{0:T(512)(128)(4,1)S(1)} %get-tuple-element.32) | copy-start | bytes 76
  13.5 77.9 %copy-start.18 = (pred[24]{0:T(512)(128)(4,1)}, pred[24]{0:T(512)(128)(4,1)S(1)}, u32[]{:S(2)}) copy-start(pred[24]{0:T(512)(128)(4,1)S(1)} %get-tuple-element.34) | copy-start | bytes 76
  16.0 143.2 %copy-start.20 = (pred[24]{0:T(512)(128)(4,1)}, pred[24]{0:T(512)(128)(4,1)S(1)}, u32[]{:S(2)}) copy-start(pred[24]{0:T(512)(128)(4,1)S(1)} %get-tuple-element.15) | copy-start | bytes 76
  87.6 0.9 copy-start.2
  162.2 1.8 copy-start.1
  168.4 0.9 copy-start.6
  170.2 0.9 copy-start.16
  171.0 2.1 copy-start.7
  174.1 13.1 %copy-start.11 = (f32[24,32]{1,0:T(8,128)S(1)}, f32[24,32]{1,0:T(8,128)}, u32[]{:S(2)}) copy-start(f32[24,32]{1,0:T(8,128)} %fusion.24) | copy-start | bytes 9220
  202.5 9.1 %copy-start.3 = (bf16[24,128,128]{2,1,0:T(8,128)(2,1)S(1)}, bf16[24,128,128]{2,1,0:T(8,128)(2,1)}, u32[]{:S(2)}) copy-start(bf16[24,128,128]{2,1,0:T(8,128)(2,1)} %copy-done.2) | copy-start | bytes 2359300
  202.5 9.1 %copy-start.13 = (pred[24]{0:T(512)(128)(4,1)S(1)}, pred[24]{0:T(512)(128)(4,1)}, u32[]{:S(2)}) copy-start(pred[24]{0:T(512)(128)(4,1)} %copy-done.12) | copy-start | bytes 76
  202.5 9.1 %copy-start.15 = (pred[24]{0:T(512)(128)(4,1)S(1)}, pred[24]{0:T(512)(128)(4,1)}, u32[]{:S(2)}) copy-start(pred[24]{0:T(512)(128)(4,1)} %copy-done.14) | copy-start | bytes 76
  202.5 147.2 %all-to-all-start = ((bf16[128,32,128]{2,0,1:T(8,128)(2,1)}), bf16[128,32,128]{2,0,1:T(8,128)(2,1)S(1)}, u32[]{:S(2)}, u32[]{:S(2)}) async-start(bf16[128,32,128]{2,0,1:T(8,128)(2,1)} %copy.69), calls=%async_computation | async-start | bytes 2097152 | tf_op jit(solution)/shard_map/all_to_all | solution.py:95
  211.5 2.7 copy-start.4
  211.5 2.7 copy-start.17
  211.5 133.9 %all-reduce.6.cloned.1.call-start = ((), (), s32[]{:S(2)}) async-start(), calls=%async_computation.3 | async-start | bytes 4718592
  211.6 2.7 copy-start.8
  211.6 2.6 copy-start.19
  215.7 1.1 copy-start.5
  215.7 1.1 copy-start.21
  215.7 1.1 copy-start.25
  216.8 1.1 copy-start.9
  216.8 1.1 copy-start.22
  217.4 1.7 copy-start.10
  217.4 1.7 copy-start.23
  218.0 2.2 copy-start.24
Sparse Core Ops, SparseCore 0:
  10.7 74.5 all-gather.4
  87.9 67.8 all-gather.2
  221.5 123.9 all-reduce.5
where the time goes:
time: 358 us; the launch traced here: 357 us
  waiting for transfers between devices  249 us (70%)
  other arithmetic  44.7 us (12%)
  local copies, waits for them, and re-layouts  27.3 us (8%)
  between operations  14.8 us (4%)
  matrix products  11.6 us (3%)
  starting transfers between devices  9.13 us (3%)
    unnamed x4, waiting for transfers between devices  122 us
    all_gather x1, waiting for transfers between devices, on_device(): lax.all_gather(inputs, 'tensor', axis=1, tiled=True)  66.7 us
    all_gather x1, waiting for transfers between devices, on_device(): lax.all_gather(cotangent, 'tensor', axis=1, tiled=True)  60.6 us
    reduce_sum x4, other arithmetic, select_sum(): return jnp.sum(values[:, :, None, :] * table[None, :, :, None], axis=1)  31.7 us
    unnamed x58, local copies, waits for them, and re-layouts  10.7 us
    all_to_all x1, starting transfers between devices, on_device(): lax.all_to_all(pieces, 'tensor', split_axis=1, concat_axis=1, tiled=True)  9 us
  transfers between devices with their start and end apart: 4, of which 3 were waited for; matrix products, arithmetic and copies ran while one was open for 9% of the time, Pallas kernels for 0%

commit v1 on v0

--- a/solution.py
+++ b/solution.py
@@ -51,7 +51,9 @@
     down_live, down_feat, down_row = decode(down_list[0], hidden_rows)
     whole_in, whole_cot = (
         lax.all_gather(inputs, "tensor", axis=1, tiled=True),
-        lax.all_gather(cotangent, "tensor", axis=1, tiled=True),
+        jnp.concatenate(
+            lax.all_to_all(jnp.stack([cotangent] * lax.axis_size("tensor")), "tensor", 0, 0), axis=1
+        ),
     )
     input_blocks = whole_in.reshape(tokens_here, feat_blocks, BLOCK)
     gate_in = jnp.take(input_blocks, gate_feat, axis=1)

time: 358 us -> 302 us (0.84)
  waiting for transfers between devices: 249 us -> 185 us
  starting transfers between devices: 9.13 us -> 24.5 us
  other arithmetic: 44.7 us -> 40.4 us
    all_gather x1 -> x0, waiting for transfers between devices: 60.6 us -> none  [on_device(): lax.all_gather(cotangent, 'tensor', axis=1, tiled=True)]
    all_to_all x0 -> x1, starting transfers between devices: none -> 15.4 us  [on_device(): lax.all_to_all(jnp.stack([cotangent] * lax.axis_size('tensor')), 'tensor'...]
    unnamed x58 -> x65, local copies, waits for them, and re-layouts: 10.7 us -> 9.42 us
    unnamed x4 -> x3, waiting for transfers between devices: 122 us -> 122 us
  transfers between devices with their start and end apart: 4 -> 4, of which waited for: 3 -> 2; matrix products, arithmetic and copies ran while one was open for 9% -> 10% of each run, Pallas kernels for 0% -> 0%
where the time goes in v1:
time: 302 us
  waiting for transfers between devices  185 us (61%)
  other arithmetic  40.4 us (13%)
  local copies, waits for them, and re-layouts  25.7 us (9%)
  starting transfers between devices  24.5 us (8%)
  between operations  15.2 us (5%)
  matrix products  10.3 us (3%)
    unnamed x3, waiting for transfers between devices  122 us
    all_gather x1, waiting for transfers between devices, on_device(): lax.all_gather(inputs, 'tensor', axis=1, tiled=True)  63.1 us
    reduce_sum x4, other arithmetic, select_sum(): return jnp.sum(values[:, :, None, :] * table[None, :, :, None], axis=1)  31.5 us
    all_to_all x1, starting transfers between devices, on_device(): lax.all_to_all(jnp.stack([cotangent] * lax.axis_size('tensor')), 'tensor'...  15.4 us
    unnamed x65, local copies, waits for them, and re-layouts  9.42 us
    all_to_all x1, starting transfers between devices, on_device(): lax.all_to_all(pieces, 'tensor', split_axis=1, concat_axis=1, tiled=True)  9.03 us
  transfers between devices with their start and end apart: 4, of which 2 were waited for; matrix products, arithmetic and copies ran while one was open for 10% of the time, Pallas kernels for 0%

profile of v1, /device:TPU:32, one launch (start us, length us, event | category | flops | bytes accessed | tf_op | source)
XLA Modules:
  0.0 301.7 jit_solution(7538096695130679157)
XLA Ops:
  7.2 0.0 copy-start
  7.2 0.0 all-gather.2.cloned.1.call-start
  7.2 1.5 copy.50
  8.8 0.0 all-gather.2.cloned.1.call-update
  8.8 0.0 copy-start.26
  8.8 0.0 copy-start.27
  8.8 0.0 copy-start.28
  8.8 2.0 stack.2
  10.8 15.4 %all-to-all-start = ((bf16[32,128,128]{2,1,0:T(8,128)(2,1)}), bf16[32,128,128]{2,1,0:T(8,128)(2,1)}, u32[]{:S(2)}, u32[]{:S(2)}) async-start(bf16[32,128,128]{2,1,0:T(8,128)(2,1)} %stack.2), calls=%async_computation | async-start | bytes 2097152 | tf_op jit(solution)/shard_map/all_to_all | solution.py:55
  26.3 0.5 compare_and_fusion.2
  26.8 0.5 compare_and_fusion.5
  27.4 0.6 pad_clamp_fusion.2
  28.0 0.6 fusion.45
  28.6 0.5 fusion.46
  29.2 0.5 fusion.44
  29.7 0.1 fusion.26
  29.8 0.7 fusion.24
  30.5 63.1 %all-gather.2.cloned.1.call-done = bf16[128,4096]{0,1:T(8,128)(2,1)} async-done(((bf16[128,128]{0,1:T(8,128)(2,1)}), bf16[128,4096]{0,1:T(8,128)(2,1)}) %all-gather.2.cloned.1.call-update) | async-done | bytes 1048592 | tf_op jit(solution)/shard_map/all_gather | solution.py:53
  93.5 1.6 copy.51
  95.2 0.7 gather_fusion.1
  95.9 0.9 copy-done.1
  96.8 0.4 convolution_bitcast_fusion.3
  97.2 0.9 copy.52
  98.1 1.6 gather_fusion.2
  99.7 1.8 convolution_bitcast_fusion.2
  101.5 0.9 copy.56
  102.4 3.5 %multiply_reduce_fusion.2 = (f32[128,4,128]{2,1,0:T(4,128)S(1)}, f32[128,4,128]{2,1,0:T(4,128)S(1)}) fusion(f32[24,4]{0,1:T(4,128)S(1)} %fusion.32, f32[128,24,128]{2,1,0:T(8,128)S(1)} %copy.56, f32[24,4]{0,1:T(4,128)S(1)} %fusion.30, f32[128,24,128]{2,1,0:T(8,128)S(1)} %copy.52), kind=kLoop, calls=%fused_computation.8 | loop fusion | flops 6160384 | bytes 3670784 | tf_op jit(solution)/shard_map/reduce_sum | solution.py:25
  105.9 2.0 gather_fusion
  108.0 0.7 convolution_bitcast_fusion.4
  108.7 0.1 copy-done.4
  108.8 0.9 copy.49
  109.7 1.8 multiply_reduce_fusion.4
  111.5 0.2 multiply_convert_fusion.6
  111.7 0.7 gather_fusion.4
  112.4 0.7 convolution_bitcast_fusion
  113.1 0.2 copy-done.6
  113.3 0.9 copy.62
  114.2 0.0 copy-start.19
  114.2 1.0 gather_fusion.3
  115.2 2.1 convolution_bitcast_fusion.1
  117.3 1.1 copy.59
  118.4 0.0 copy-start.12
  118.5 13.1 %multiply_reduce_fusion = f32[128,32,128]{2,1,0:T(8,128)S(1)} fusion(f32[24,32]{1,0:T(8,128)S(1)} %fusion.26, f32[128,24,128]{2,1,0:T(8,128)S(1)} %copy.62), kind=kLoop, calls=%fused_computation.6 | loop fusion | flops 24641536 | bytes 3673088 | tf_op jit(solution)/shard_map/reduce_sum | solution.py:25
  131.6 13.1 %multiply_reduce_fusion.1 = f32[128,32,128]{2,1,0:T(8,128)S(1)} fusion(f32[24,32]{1,0:T(8,128)S(1)} %copy-done.12, f32[128,24,128]{2,1,0:T(8,128)S(1)} %copy.59), kind=kLoop, calls=%fused_computation.7 | loop fusion | flops 24641536 | bytes 3673088 | tf_op jit(solution)/shard_map/reduce_sum | solution.py:25
  144.7 0.5 add_convert_fusion
  145.2 1.4 copy.63
  146.6 9.0 %all-to-all-start.1 = ((bf16[128,32,128]{2,0,1:T(8,128)(2,1)}), bf16[128,32,128]{2,0,1:T(8,128)(2,1)S(1)}, u32[]{:S(2)}, u32[]{:S(2)}) async-start(bf16[128,32,128]{2,0,1:T(8,128)(2,1)} %copy.63), calls=%async_computation.1 | async-start | bytes 2097152 | tf_op jit(solution)/shard_map/all_to_all | solution.py:97
  155.7 0.0 all-reduce.6.cloned.1.call-start
  155.8 2.7 multiply_convert_fusion.3
  158.4 1.4 multiply_convert_fusion.5
  159.9 0.7 gather_fusion.5
  160.6 0.4 copy-done.5
  161.0 0.5 multiply_convert_fusion.1
  161.5 0.6 copy-done.9
  162.1 1.1 fusion.1
  163.2 1.1 fusion
  164.4 1.1 fusion.2
  165.5 0.0 all-reduce.6.cloned.1.call-update
  165.5 1.3 dynamic-slice
  167.5 122.4 %all-reduce.6.cloned.1.call-done = (bf16[1,24,128,128]{3,2,1,0:T(8,128)(2,1)}, bf16[1,24,128,128]{3,2,1,0:T(8,128)(2,1)}, bf16[1,24,128,128]{3,2,1,0:T(8,128)(2,1)}) async-done(((bf16[1,24,128,128]{3,2,1,0:T(8,128)(2,1)}, bf16[1,24,128,128]{3,2,1,0:T(8,128)(2,1)}, bf16[1,24,128,128]{3,2,1,0:T(8,128)(2,1)}), (bf16[1,24,128,128]{3,2,1,0:T(8,128)(2,1)}, bf16[1,24,128,128]{3,2,1,0:T(8,128)(2,1)}, ...) | async-done | bytes 2359312
  289.8 1.4 constant_dynamic-slice_fusion
  291.2 1.4 constant_dynamic-slice_fusion.1
  292.7 1.4 constant_dynamic-slice_fusion.2
  294.1 0.8 reduce_sum.62
  (65 shorter events, 0.2 us)
Async XLA Ops:
  7.2 89.6 %copy-start = (bf16[1,24,128,128]{3,2,1,0:T(8,128)(2,1)S(1)}, bf16[1,24,128,128]{3,2,1,0:T(8,128)(2,1)}, u32[]{:S(2)}) copy-start(bf16[1,24,128,128]{3,2,1,0:T(8,128)(2,1)} %param.15) | copy-start | bytes 2359300
  7.2 86.4 %all-gather.2.cloned.1.call-start = ((), (), s32[]{:S(2)}) async-start(), calls=%async_computation.2 | async-start | bytes 1081344 | tf_op jit(solution)/shard_map/all_gather | solution.py:53
  8.8 17.4 %copy-start.26 = (s32[1,24]{1,0:T(1,128)S(1)}, s32[1,24]{1,0:T(1,128)}, u32[]{:S(2)}) copy-start(s32[1,24]{1,0:T(1,128)} %param.18) | copy-start | bytes 292
  8.8 17.5 %copy-start.27 = (s32[1,24]{1,0:T(1,128)S(1)}, s32[1,24]{1,0:T(1,128)}, u32[]{:S(2)}) copy-start(s32[1,24]{1,0:T(1,128)} %param.17) | copy-start | bytes 292
  8.8 18.0 %copy-start.28 = (s32[1,24]{1,0:T(1,128)S(1)}, s32[1,24]{1,0:T(1,128)}, u32[]{:S(2)}) copy-start(s32[1,24]{1,0:T(1,128)} %param.19) | copy-start | bytes 292
  10.8 95.1 %all-to-all-start = ((bf16[32,128,128]{2,1,0:T(8,128)(2,1)}), bf16[32,128,128]{2,1,0:T(8,128)(2,1)}, u32[]{:S(2)}, u32[]{:S(2)}) async-start(bf16[32,128,128]{2,1,0:T(8,128)(2,1)} %stack.2), calls=%async_computation | async-start | bytes 2097152 | tf_op jit(solution)/shard_map/all_to_all | solution.py:55
  26.2 69.6 %copy-start.13 = (pred[24]{0:T(512)(128)(4,1)}, pred[24]{0:T(512)(128)(4,1)S(1)}, u32[]{:S(2)}) copy-start(pred[24]{0:T(512)(128)(4,1)S(1)} %get-tuple-element.17) | copy-start | bytes 76
  26.2 86.2 %copy-start.15 = (pred[24]{0:T(512)(128)(4,1)}, pred[24]{0:T(512)(128)(4,1)S(1)}, u32[]{:S(2)}) copy-start(pred[24]{0:T(512)(128)(4,1)S(1)} %get-tuple-element.32) | copy-start | bytes 76
  26.8 72.9 %copy-start.21 = (pred[24]{0:T(512)(128)(4,1)}, pred[24]{0:T(512)(128)(4,1)S(1)}, u32[]{:S(2)}) copy-start(pred[24]{0:T(512)(128)(4,1)S(1)} %get-tuple-element.34) | copy-start | bytes 76
  27.4 80.6 %copy-start.17 = (pred[24]{0:T(512)(128)(4,1)}, pred[24]{0:T(512)(128)(4,1)S(1)}, u32[]{:S(2)}) copy-start(pred[24]{0:T(512)(128)(4,1)S(1)} %get-tuple-element.15) | copy-start | bytes 76
  95.9 0.9 copy-start.1
  105.9 2.0 copy-start.11
  107.9 0.9 copy-start.4
  112.4 0.9 copy-start.6
  114.2 1.0 copy-start.19
  115.2 2.1 copy-start.7
  118.4 13.1 %copy-start.12 = (f32[24,32]{1,0:T(8,128)S(1)}, f32[24,32]{1,0:T(8,128)}, u32[]{:S(2)}) copy-start(f32[24,32]{1,0:T(8,128)} %fusion.24) | copy-start | bytes 9220
  146.6 9.1 %copy-start.2 = (bf16[24,128,128]{2,1,0:T(8,128)(2,1)S(1)}, bf16[24,128,128]{2,1,0:T(8,128)(2,1)}, u32[]{:S(2)}) copy-start(bf16[24,128,128]{2,1,0:T(8,128)(2,1)} %copy-done.1) | copy-start | bytes 2359300
  146.6 9.1 %copy-start.14 = (pred[24]{0:T(512)(128)(4,1)S(1)}, pred[24]{0:T(512)(128)(4,1)}, u32[]{:S(2)}) copy-start(pred[24]{0:T(512)(128)(4,1)} %copy-done.13) | copy-start | bytes 76
  146.6 9.1 %copy-start.16 = (pred[24]{0:T(512)(128)(4,1)S(1)}, pred[24]{0:T(512)(128)(4,1)}, u32[]{:S(2)}) copy-start(pred[24]{0:T(512)(128)(4,1)} %copy-done.15) | copy-start | bytes 76
  146.6 147.5 %all-to-all-start.1 = ((bf16[128,32,128]{2,0,1:T(8,128)(2,1)}), bf16[128,32,128]{2,0,1:T(8,128)(2,1)S(1)}, u32[]{:S(2)}, u32[]{:S(2)}) async-start(bf16[128,32,128]{2,0,1:T(8,128)(2,1)} %copy.63), calls=%async_computation.1 | async-start | bytes 2097152 | tf_op jit(solution)/shard_map/all_to_all | solution.py:97
  155.6 2.8 copy-start.3
  155.7 2.8 copy-start.20
  155.7 134.1 %all-reduce.6.cloned.1.call-start = ((), (), s32[]{:S(2)}) async-start(), calls=%async_computation.3 | async-start | bytes 4718592
  155.7 2.7 copy-start.8
  155.8 2.7 copy-start.22
  159.8 1.1 copy-start.5
  159.9 1.1 copy-start.18
  159.9 1.1 copy-start.29
  161.0 1.1 copy-start.9
  161.0 1.1 copy-start.25
  161.5 1.7 copy-start.10
  161.5 1.7 copy-start.24
  162.1 2.2 copy-start.23
Sparse Core Ops, SparseCore 0:
  10.7 82.8 all-gather.1
  165.6 124.1 all-reduce.5
